TPU v7x, 32 devices: a whole 2x2x4 slice. The times are simulated.
32 devices in a mesh: teacher: 4 (over y, x), vocab: 8 (over z, core).
Axes of the slice: x: 2, y: 2, z: 4, core: 2. Of those that a mesh axis runs over, the one named last changes fastest.
Arguments:
- teacher_hidden: bfloat16 [4, 1024, 4096], P('teacher', 'vocab'), may hold values from -180 to 180
- teacher_head: bfloat16 [4, 4096, 32000], P('teacher', None, 'vocab'), may hold values from -0.375 to 0.375
- student_hidden: bfloat16 [1024, 4096], P('teacher'), may hold values from -180 to 180
- student_head: bfloat16 [4096, 32000], P('teacher', 'vocab'), may hold values from -0.375 to 0.375
Outputs:
- loss: float32 [], replicated
- grad_hidden: float32 [1024, 4096], P('teacher', 'vocab')
- grad_weight: float32 [4096, 32000], P('teacher', 'vocab')
All inputs are finite; a program needn't handle non-finite values.
Results may differ from a plain program's by a relative error of at most 0.0027.
Values may be sent and summed in bfloat16 or wider, within the bound.
A program may use at most 192 MiB of HBM per device.

v0:
```python
import jax
import jax.numpy as jnp
from jax import lax
from jax.sharding import PartitionSpec as P

TOK = 1024


def teacher_stats(logits):
    local_top = jnp.max(logits, axis=-1)
    top = lax.pmax(local_top, "vocab")
    shifted = jnp.exp(logits - top[:, None])
    total, moment = lax.psum(
        (jnp.sum(shifted, axis=-1), jnp.sum(shifted * logits, axis=-1)), "vocab"
    )
    return (top, total, moment)


def paired_lse(stacked):
    local_top = jnp.max(stacked, axis=-1)
    top = lax.pmax(local_top, "vocab")
    total = lax.psum(jnp.sum(jnp.exp(stacked - top[..., None]), axis=-1), "vocab")
    return top + jnp.log(total)


def per_device(teacher_hidden, teacher_head, student_hidden, student_head):
    head = teacher_head[0]
    logits = jnp.dot(
        lax.all_gather(teacher_hidden[0], "vocab", axis=0, tiled=True),
        head,
        preferred_element_type=jnp.float32,
    )
    top, total, moment = teacher_stats(logits)
    lse = top + jnp.log(total)
    entropy = lse - moment / total
    confid = jnp.exp(-entropy)
    weighted = confid[:, None] * (logits - lse[:, None])
    wsum, csum = (
        lax.psum_scatter(weighted, "teacher", scatter_dimension=0, tiled=True),
        lax.psum_scatter(confid, "teacher", scatter_dimension=0, tiled=True),
    )
    raw = wsum / csum[:, None]
    full_head = lax.all_gather(student_head, "teacher", axis=0, tiled=True)
    slog = jnp.dot(student_hidden, full_head, preferred_element_type=jnp.float32)
    both_lse = paired_lse(jnp.stack([raw, slog]))
    target = raw - both_lse[0][:, None]
    slp = slog - both_lse[1][:, None]
    probs = jnp.exp(target)
    partial_kl = jnp.sum(probs * (target - slp))
    loss = lax.psum(partial_kl, ("teacher", "vocab")) / TOK
    gradl = (jnp.exp(slp) - probs).astype(jnp.bfloat16)
    grad_hidden = lax.psum_scatter(
        lax.dot_general(
            full_head, gradl, (((1,), (1,)), ((), ())), preferred_element_type=jnp.float32
        ),
        "vocab",
        scatter_dimension=0,
        tiled=True,
    ).T
    columns = lax.all_to_all(student_hidden, "teacher", split_axis=1, concat_axis=0, tiled=True)
    all_grads = lax.all_gather(gradl, "teacher", axis=0, tiled=True)
    grad_weight = lax.dot_general(
        columns, all_grads, (((0,), (0,)), ((), ())), preferred_element_type=jnp.float32
    )
    return (loss, grad_hidden, grad_weight)


def solution(mesh):
    placed = (
        P("teacher", "vocab", None),
        P("teacher", None, "vocab"),
        P("teacher", None),
        P("teacher", "vocab"),
    )
    return jax.shard_map(
        per_device,
        mesh=mesh,
        in_specs=placed,
        out_specs=(P(), P("teacher", "vocab"), P("teacher", "vocab")),
        check_vma=False,
    )
```

profile of v0, /device:TPU:3, one launch (start us, length us, event | category | flops | bytes accessed | tf_op | source)
XLA Modules:
  0.0 846.0 jit_solution(5529223192047300215)
XLA Ops:
  7.2 0.7 all-gather.9.cloned.1.call-update
  7.9 0.0 reduce-scatter.3.cloned.1.call-start
  7.9 85.4 %all-gather.9.cloned.1.call-done = bf16[1,1024,4096]{2,1,0:T(8,128)(2,1)} async-done(((bf16[1,128,4096]{2,1,0:T(8,128)(2,1)}), bf16[1,1024,4096]{2,1,0:T(8,128)(2,1)}) %all-gather.9.cloned.1.call-update) | async-done | bytes 8388624 | tf_op jit(solution)/shard_map/all_gather | solution.py:29
  93.4 41.8 %fusion.7 = (f32[1024]{0:T(1024)S(1)}, f32[1024,4000]{0,1:T(8,128)}) fusion(bf16[1,4096,4000]{1,2,0:T(8,128)(2,1)} %param.5, bf16[1,1024,4096]{2,1,0:T(8,128)(2,1)} %all-gather.9.cloned.1.call-done), kind=kOutput, calls=%fused_computation.20 | convolution fusion | flops 33558528000 | bytes 57544704 | tf_op jit(solution)/shard_map/dot_general | solution.py:28
  135.2 13.2 %pmax.14 = f32[1024]{0:T(1024)S(1)} all-reduce(f32[1024]{0:T(1024)S(1)} %get-tuple-element.13), channel_id=1, replica_groups=mesh['teacher'=4,'vocab'=8] {'vocab'}, use_global_device_ids=true, to_apply=%region_1.0 | all-reduce | flops 1024 | bytes 8192 | tf_op jit(solution)/shard_map/pmax | solution.py:11
  148.4 7.6 multiply_reduce_fusion
  156.0 14.4 %all-reduce.1 = (f32[1024]{0:T(1024)S(1)}, f32[1024]{0:T(1024)S(1)}) all-reduce(f32[1024]{0:T(1024)S(1)} %get-tuple-element.4, f32[1024]{0:T(1024)S(1)} %get-tuple-element.3), channel_id=1, replica_groups=mesh['teacher'=4,'vocab'=8] {'vocab'}, use_global_device_ids=true, to_apply=%region_3.0 | all-reduce | flops 2048 | bytes 16384 | tf_op jit(solution)/shard_map/psum | solution.py:13
  170.4 11.5 %subtract_multiply_fusion = f32[1024,4000]{0,1:T(8,128)} fusion(f32[1024,4000]{0,1:T(8,128)} %get-tuple-element.14, f32[1024]{0:T(1024)S(1)} %get-tuple-element.10, f32[1024]{0:T(1024)S(1)} %get-tuple-element.9), kind=kLoop, calls=%fused_computation.2 | loop fusion | flops 8192000 | bytes 32776192 | tf_op jit(solution)/shard_map/mul | solution.py:37
  182.0 0.0 all-gather.5.cloned.1.call-start
  182.0 0.7 all-gather.5.cloned.1.call-update
  182.8 0.6 dynamic-slice
  184.0 6.5 all-reduce
  190.5 0.1 dynamic-slice.1
  190.6 140.2 %reduce-scatter.3.cloned.1.call-done = f32[256,4000]{0,1:T(8,128)} async-done(((f32[1024,4000]{0,1:T(8,128)}), f32[256,4000]{0,1:T(8,128)}) %reduce-scatter.3.cloned.1.call-update) | async-done | bytes 4096016 | tf_op jit(solution)/shard_map/reduce_scatter | solution.py:39
  330.8 4.4 fusion.5
  335.2 288.5 %all-gather.5.cloned.1.call-done = bf16[4096,4000]{0,1:T(8,128)(2,1)} async-done(((bf16[1024,4000]{0,1:T(8,128)(2,1)}), bf16[4096,4000]{0,1:T(8,128)(2,1)}) %all-gather.5.cloned.1.call-update) | async-done | bytes 32768016 | tf_op jit(solution)/shard_map/all_gather | solution.py:43
  623.7 14.1 %fusion.8 = f32[256,4000]{0,1:T(8,128)S(1)} fusion(bf16[256,4096]{1,0:T(8,128)(2,1)S(1)} %copy-done.2, bf16[4096,4000]{0,1:T(8,128)(2,1)} %all-gather.5.cloned.1.call-done), kind=kOutput, calls=%fused_computation.21 | convolution fusion | flops 8388608000 | bytes 38961152 | tf_op jit(solution)/shard_map/dot_general | solution.py:44
  637.8 2.0 copy-done.1
  639.8 0.6 fusion.4
  640.4 13.6 %pmax.15 = f32[2,256]{1,0:T(2,128)S(1)} all-reduce(f32[2,256]{1,0:T(2,128)S(1)} %fusion.4), channel_id=1, replica_groups=mesh['teacher'=4,'vocab'=8] {'vocab'}, use_global_device_ids=true, to_apply=%region_9.0 | all-reduce | flops 512 | bytes 4096 | tf_op jit(solution)/shard_map/pmax | solution.py:21
  654.0 4.0 exponential_reduce_fusion
  657.9 16.6 %psum.30 = f32[2,256]{1,0:T(2,128)S(1)} all-reduce(f32[2,256]{1,0:T(2,128)S(1)} %exponential_reduce_fusion), channel_id=1, replica_groups=mesh['teacher'=4,'vocab'=8] {'vocab'}, use_global_device_ids=true, to_apply=%region_11.0 | all-reduce | flops 512 | bytes 4096 | tf_op jit(solution)/shard_map/psum | solution.py:22
  674.5 6.9 subtract_convert_fusion
  681.5 0.0 reduce-scatter.5.cloned.1.call-start
  681.5 18.8 %convolution_bitcast_fusion.1 = f32[4096,256]{0,1:T(8,128)} fusion(bf16[256,4000]{0,1:T(8,128)(2,1)} %get-tuple-element.7, bf16[4096,4000]{0,1:T(8,128)(2,1)} %all-gather.5.cloned.1.call-done), kind=kOutput, calls=%fused_computation.11 | convolution fusion | flops 8388608000 | bytes 39010304 | tf_op jit(solution)/shard_map/dot_general | solution.py:53
  700.3 2.5 copy.9
  702.8 32.5 %all_to_all.19 = bf16[256,4,1024]{0,2,1:T(8,128)(2,1)S(1)} all-to-all(bf16[256,4,1024]{0,2,1:T(8,128)(2,1)} %bitcast.33), channel_id=1, replica_groups=mesh['teacher'=4,'vocab'=8] {'teacher'}, dimensions={1} | all-to-all | bytes 4194304 | tf_op jit(solution)/shard_map/all_to_all | solution.py:60
  735.3 2.5 copy.10
  737.8 40.2 %psum.31 = f32[]{:T(128)} all-reduce(f32[]{:T(128)} %get-tuple-element.8), channel_id=1, replica_groups=mesh['teacher'=4,'vocab'=8] {'teacher','vocab'}, use_global_device_ids=true, to_apply=%region_13.0 | all-reduce | flops 1 | bytes 8 | tf_op jit(solution)/shard_map/psum | solution.py:50
  778.6 8.9 %all-gather.7.cloned.1.call-done = bf16[1024,4000]{0,1:T(8,128)(2,1)} async-done(((bf16[256,4000]{0,1:T(8,128)(2,1)}), bf16[1024,4000]{0,1:T(8,128)(2,1)}) %all-gather.7.cloned.1.call-update) | async-done | bytes 8192016 | tf_op jit(solution)/shard_map/all_gather | solution.py:61
  787.6 15.9 %convolution_bitcast_fusion = f32[1024,4000]{0,1:T(8,128)} fusion(bf16[1024,4000]{0,1:T(8,128)(2,1)} %all-gather.7.cloned.1.call-done, bf16[1024,1024]{1,0:T(8,128)(2,1)} %bitcast.34), kind=kOutput, calls=%fused_computation.6 | convolution fusion | flops 8388608000 | bytes 26673152 | tf_op jit(solution)/shard_map/dot_general | solution.py:62
  803.4 34.9 %reduce-scatter.5.cloned.1.call-done = f32[512,256]{0,1:T(8,128)} async-done(((f32[4096,256]{0,1:T(8,128)}), f32[512,256]{0,1:T(8,128)}) %reduce-scatter.5.cloned.1.call-update) | async-done | bytes 524304 | tf_op jit(solution)/shard_map/reduce_scatter | solution.py:52
  (15 shorter events, 0.2 us)
Async XLA Ops:
  7.2 86.2 %all-gather.9.cloned.1.call-start = ((), (), s32[]{:S(2)}) async-start(), calls=%async_computation.7 | async-start | bytes 9437184 | tf_op jit(solution)/shard_map/all_gather | solution.py:29
  7.9 322.9 %reduce-scatter.3.cloned.1.call-start = ((), (), s32[]{:S(2)}) async-start(), calls=%async_computation.3 | async-start | bytes 20480000 | tf_op jit(solution)/shard_map/reduce_scatter | solution.py:39
  181.9 0.8 copy-start.3
  182.0 441.7 %copy-start.2 = (bf16[256,4096]{1,0:T(8,128)(2,1)S(1)}, bf16[256,4096]{1,0:T(8,128)(2,1)}, u32[]{:S(2)}) copy-start(bf16[256,4096]{1,0:T(8,128)(2,1)} %param.6) | copy-start | bytes 6291460
  182.0 441.7 %all-gather.5.cloned.1.call-start = ((), (), s32[]{:S(2)}) async-start(), calls=%async_computation.4 | async-start | bytes 40960000 | tf_op jit(solution)/shard_map/all_gather | solution.py:43
  182.7 604.9 %all-gather.7.cloned.1.call-start = ((), (), s32[]{:S(2)}) async-start(), calls=%async_computation.6 | async-start | bytes 10240000 | tf_op jit(solution)/shard_map/all_gather | solution.py:61
  623.7 16.1 %copy-start = (f32[1,256,4000]{1,2,0:T(8,128)S(1)}, f32[1,256,4000]{1,2,0:T(8,128)}, u32[]{:S(2)}) copy-start(f32[1,256,4000]{1,2,0:T(8,128)} %fusion.5) | copy-start | bytes 12288004
  637.8 2.0 copy-start.1
  681.5 156.8 %reduce-scatter.5.cloned.1.call-start = ((), (), s32[]{:S(2)}) async-start(), calls=%async_computation.5 | async-start | bytes 4718592 | tf_op jit(solution)/shard_map/reduce_scatter | solution.py:52
Sparse Core Ops, SparseCore 0:
  9.6 83.7 all-gather.8
  182.1 148.6 reduce-scatter.2
  332.8 290.7 all-gather.4
  681.6 105.9 all-gather.6
  790.4 47.8 reduce-scatter.4
where the time goes:
time: 850 us; the launch traced here: 846 us
  waiting for transfers between devices  559 us (66%)
  blocking collectives  137 us (16%)
  matrix products  90.6 us (11%)
  other arithmetic  34.9 us (4%)
  between operations  16.3 us (2%)
    all_gather x1, waiting for transfers between devices, per_device(): full_head = lax.all_gather(student_head, 'teacher', axis=0, tiled=True)  288 us
    reduce_scatter x1, waiting for transfers between devices, per_device(): lax.psum_scatter(weighted, 'teacher', scatter_dimension=0, tiled=True)  140 us
    all_gather x1, waiting for transfers between devices, per_device(): lax.all_gather(teacher_hidden[0], 'vocab', axis=0, tiled=True)  85.4 us
    dot_general x1, matrix products, per_device(): jnp.dot(lax.all_gather(teacher_hidden[0], 'vocab', axis=0, tiled=True), h...  41.8 us
    psum x1, blocking collectives, per_device(): loss = lax.psum(partial_kl, ('teacher', 'vocab')) / TOK  40.2 us
    reduce_scatter x1, waiting for transfers between devices, per_device(): lax.psum_scatter(lax.dot_general(full_head, gradl, (((1,), (1,)), ((), ()...  34.9 us
    all_to_all x1, blocking collectives, per_device(): lax.all_to_all(student_hidden, 'teacher', split_axis=1, concat_axis=0, ti...  32.5 us
    dot_general x1, matrix products, per_device(): lax.dot_general(full_head, gradl, (((1,), (1,)), ((), ())), preferred_ele...  18.8 us
  transfers between devices with their start and end apart: 5, of which 5 were waited for; matrix products, arithmetic and copies ran while one was open for 5% of the time, Pallas kernels for 0%

commit v1 on v0

v1 whole, which is shorter than its diff:
```python
import functools

import jax
import jax.numpy as jnp
from jax import lax
from jax.experimental import pallas as pl
from jax.experimental.pallas import tpu as pltpu
from jax.sharding import PartitionSpec as P

F32 = jnp.float32


def gather_hidden(own, nv, first):
    chips = nv // 2
    at = lax.axis_index("vocab")
    chip = at // 2
    up = [own]
    down = [own]
    for hop in range(chips - 1):
        up.append(lax.ppermute(up[-1], "vocab", [(i, i + 2) for i in range(nv - 2)]))
        down.append(lax.ppermute(down[-1], "vocab", [(i + 2, i) for i in range(nv - 2)]))
        if hop == 0:
            up[-1], down[-1], first = lax.optimization_barrier((up[-1], down[-1], first))
    pair = [(i, i ^ 1) for i in range(nv)]
    rows, width = own.shape
    buf = jnp.zeros((chips, 2, rows, width), own.dtype)
    core = at % 2
    for k in range(chips):
        piece = own if k == 0 else up[k] + down[chips - k]
        other = lax.ppermute(piece, "vocab", pair)
        slot = lax.rem(chip - k + chips, chips)
        buf = lax.dynamic_update_slice(buf, piece[None, None], (slot, core, 0, 0))
        buf = lax.dynamic_update_slice(buf, other[None, None], (slot, 1 - core, 0, 0))
    return buf.reshape(nv * rows, width), first


def exchange_kernel(nv, own_ref, out_ref, slots, send, recv):
    me = lax.axis_index("vocab")
    barrier = pltpu.get_barrier_semaphore()
    for step in range(1, nv):
        pl.semaphore_signal(
            barrier,
            inc=1,
            device_id={"vocab": lax.rem(me + step, nv)},
            device_id_type=pl.DeviceIdType.MESH,
        )
    pl.semaphore_wait(barrier, nv - 1)
    copies = []
    for step in range(1, nv):
        copies.append(
            pltpu.make_async_remote_copy(
                src_ref=own_ref,
                dst_ref=slots.at[me],
                send_sem=send.at[step - 1],
                recv_sem=recv.at[step - 1],
                device_id={"vocab": lax.rem(me + step, nv)},
                device_id_type=pl.DeviceIdType.MESH,
            )
        )
        copies[-1].start()
    slots[me] = own_ref[...]
    for copy in copies:
        copy.wait()
    out_ref[...] = slots[...]


def slotted(stats, nv, ident):
    return pl.pallas_call(
        functools.partial(exchange_kernel, nv),
        out_shape=jax.ShapeDtypeStruct((nv,) + stats.shape, F32),
        in_specs=[pl.BlockSpec(memory_space=pltpu.VMEM)],
        out_specs=pl.BlockSpec(memory_space=pltpu.VMEM),
        scratch_shapes=[
            pltpu.VMEM((nv,) + stats.shape, F32),
            pltpu.SemaphoreType.DMA((nv - 1,)),
            pltpu.SemaphoreType.DMA((nv - 1,)),
        ],
        compiler_params=pltpu.CompilerParams(collective_id=ident, has_side_effects=True),
    )(stats)


def per_device(nt, nv, tok, teacher_hidden, teacher_head, student_hidden, student_head):
    head = teacher_head[0]
    columns = lax.all_to_all(student_hidden, "teacher", split_axis=1, concat_axis=0, tiled=True)
    partial_slog = jnp.dot(columns, student_head, preferred_element_type=F32)
    hidden, partial_slog = gather_hidden(teacher_hidden[0], nv, partial_slog)
    slog = lax.psum_scatter(partial_slog, "teacher", scatter_dimension=0, tiled=True)

    logits = jnp.dot(hidden, head, preferred_element_type=F32)
    m = jnp.max(logits, axis=-1)
    e = jnp.exp(logits - m[:, None])
    st = slotted(jnp.stack([m, jnp.sum(e, axis=-1), jnp.sum(e * logits, axis=-1)]), nv, 0)
    top = jnp.max(st[:, 0], axis=0)
    scale = jnp.exp(st[:, 0] - top)
    total = jnp.sum(st[:, 1] * scale, axis=0)
    moment = jnp.sum(st[:, 2] * scale, axis=0)
    lse = top + jnp.log(total)
    confid = jnp.exp(moment / total - lse)
    weighted = confid[:, None] * (logits - lse[:, None])
    slog, weighted = lax.optimization_barrier((slog, weighted))
    wsum = lax.psum_scatter(weighted, "teacher", scatter_dimension=0, tiled=True)
    csum = lax.psum_scatter(confid, "teacher", scatter_dimension=0, tiled=True)

    raw = wsum / csum[:, None]
    ms = jnp.max(slog, axis=-1)
    ss = jnp.sum(jnp.exp(slog - ms[:, None]), axis=-1)
    mr = jnp.max(raw, axis=-1)
    er = jnp.exp(raw - mr[:, None])
    st = slotted(
        jnp.stack([mr, jnp.sum(er, axis=-1), jnp.sum(er * (raw - slog), axis=-1), ms, ss]), nv, 1
    )
    tr = jnp.max(st[:, 0], axis=0)
    cr = jnp.exp(st[:, 0] - tr)
    total_r = jnp.sum(st[:, 1] * cr, axis=0)
    cross = jnp.sum(st[:, 2] * cr, axis=0)
    ts = jnp.max(st[:, 3], axis=0)
    total_s = jnp.sum(st[:, 4] * jnp.exp(st[:, 3] - ts), axis=0)
    lse_r = tr + jnp.log(total_r)
    lse_s = ts + jnp.log(total_s)
    kl = cross / total_r - lse_r + lse_s
    gradl = (jnp.exp(slog - lse_s[:, None]) - jnp.exp(raw - lse_r[:, None])).astype(jnp.bfloat16)
    all_grads = lax.all_gather(gradl, "teacher", axis=0, tiled=True)
    loss = lax.psum(jnp.sum(kl), "teacher") / tok

    r = nv // nt
    feats = student_head.shape[0]
    gh = lax.dot_general(
        all_grads, student_head, (((1,), (1,)), ((), ())), preferred_element_type=F32
    )
    gh = gh.reshape(nt, tok // nt, r, feats // r).transpose(0, 2, 1, 3)
    gh = gh.reshape(nv * (tok // nt), feats // r)
    gh = lax.psum_scatter(gh, "vocab", scatter_dimension=0, tiled=True)
    swap = [
        (s * nv + t * r + c, t * nv + s * r + c)
        for s in range(nt)
        for t in range(nt)
        for c in range(r)
    ]
    grad_hidden = lax.ppermute(gh, ("teacher", "vocab"), swap)
    grad_weight = lax.dot_general(
        columns, all_grads, (((0,), (0,)), ((), ())), preferred_element_type=F32
    )
    return (loss, grad_hidden, grad_weight)


def solution(mesh):
    nt, nv = mesh.shape["teacher"], mesh.shape["vocab"]

    def whole(teacher_hidden, teacher_head, student_hidden, student_head):
        tok = student_hidden.shape[0]
        return jax.shard_map(
            lambda *a: per_device(nt, nv, tok, *a),
            mesh=mesh,
            in_specs=(
                P("teacher", "vocab", None),
                P("teacher", None, "vocab"),
                P("teacher", None),
                P("teacher", "vocab"),
            ),
            out_specs=(P(), P("teacher", "vocab"), P("teacher", "vocab")),
            check_vma=False,
        )(teacher_hidden, teacher_head, student_hidden, student_head)

    return whole
```

time: 850 us -> 625 us (0.74)
  waiting for transfers between devices: 559 us -> 382 us
  blocking collectives: 137 us -> 13.8 us
  local copies, waits for them, and re-layouts: 7.62 us -> 38.1 us
  starting transfers between devices: 0.2 us -> 30.4 us
  Pallas kernels: 0 us -> 16.1 us
    all_gather x2 -> x0, waiting for transfers between devices: 374 us -> none  [the longest x1 288 us: per_device(): full_head = lax.all_gather(student_head, 'teacher', axis=0, tiled=True)]
    ppermute x0 -> x11, waiting for transfers between devices: none -> 98.3 us  [the longest x3 40.5 us: gather_hidden(): lax.ppermute(up[-1], 'vocab', [(i, i + 2) for i in range(nv - 2)])]
    all_gather x1, waiting for transfers between devices: 8.93 us -> 85.6 us  [per_device(): all_grads = lax.all_gather(gradl, 'teacher', axis=0, tiled=True)]
    psum x3 -> x1, blocking collectives: 71.2 us -> 6.8 us  [per_device(): loss = lax.psum(jnp.sum(kl), 'teacher') / tok]
    all_to_all x1 -> x0, blocking collectives: 32.5 us -> none  [per_device(): lax.all_to_all(student_hidden, 'teacher', split_axis=1, concat_axis=0, ti...]
    pmax x2 -> x0, blocking collectives: 26.8 us -> none  [the longest x1 13.6 us: paired_lse(): top = lax.pmax(local_top, 'vocab')]
    ppermute x0 -> x11, starting transfers between devices: none -> 26.6 us  [the longest x3 12.1 us: gather_hidden(): lax.ppermute(up[-1], 'vocab', [(i, i + 2) for i in range(nv - 2)])]
    all_to_all x0 -> x1, waiting for transfers between devices: none -> 18 us  [per_device(): lax.all_to_all(student_hidden, 'teacher', split_axis=1, concat_axis=0, ti...]
  transfers between devices with their start and end apart: 5 -> 16, of which waited for: 5 -> 10; matrix products, arithmetic and copies ran while one was open for 5% -> 18% of each run, Pallas kernels for 0% -> 1%
where the time goes in v1:
time: 625 us; the launch traced here: 623 us
  waiting for transfers between devices  382 us (61%)
  matrix products  85.9 us (14%)
  other arithmetic  40.2 us (6%)
  local copies, waits for them, and re-layouts  38.1 us (6%)
  starting transfers between devices  30.4 us (5%)
  between operations  16.4 us (3%)
  Pallas kernels  16.1 us (3%)
  blocking collectives  13.8 us (2%)
    reduce_scatter x1, waiting for transfers between devices, per_device(): lax.psum_scatter(weighted, 'teacher', scatter_dimension=0, tiled=True)  139 us
    all_gather x1, waiting for transfers between devices, per_device(): all_grads = lax.all_gather(gradl, 'teacher', axis=0, tiled=True)  85.6 us
    dot_general x1, matrix products, per_device(): logits = jnp.dot(hidden, head, preferred_element_type=F32)  40.8 us
    reduce_scatter x1, waiting for transfers between devices, per_device(): gh = lax.psum_scatter(gh, 'vocab', scatter_dimension=0, tiled=True)  40.6 us
    ppermute x3, waiting for transfers between devices, gather_hidden(): lax.ppermute(up[-1], 'vocab', [(i, i + 2) for i in range(nv - 2)])  40.5 us
    ppermute x3, waiting for transfers between devices, gather_hidden(): lax.ppermute(down[-1], 'vocab', [(i + 2, i) for i in range(nv - 2)])  35.5 us
    ppermute x1, waiting for transfers between devices, per_device(): grad_hidden = lax.ppermute(gh, ('teacher', 'vocab'), swap)  20 us
    all_to_all x1, waiting for transfers between devices, per_device(): lax.all_to_all(student_hidden, 'teacher', split_axis=1, concat_axis=0, ti...  18 us
  transfers between devices with their start and end apart: 16, of which 10 were waited for; matrix products, arithmetic and copies ran while one was open for 18% of the time, Pallas kernels for 1%

profile of v1, /device:TPU:3, one launch (start us, length us, event | category | flops | bytes accessed | tf_op | source)
XLA Modules:
  0.0 622.7 jit_solution(51806320394423642)
XLA Ops:
  7.2 4.1 copy.27
  11.2 3.7 all-to-all-start
  14.9 4.3 collective-permute-start
  20.6 18.0 %all-to-all-done = bf16[256,4,1024]{0,2,1:T(8,128)(2,1)S(1)} async-done(((bf16[256,4,1024]{0,2,1:T(8,128)(2,1)}), bf16[256,4,1024]{0,2,1:T(8,128)(2,1)S(1)}, u32[]{:S(2)}, u32[]{:S(2)}) %all-to-all-start) | async-done | bytes 2097184 | tf_op jit(solution)/shard_map/all_to_all | solution.py:84
  41.0 15.8 %fusion.21 = f32[1024,4000]{0,1:T(8,128)} fusion(bf16[1024,1024]{1,0:T(8,128)(2,1)} %bitcast.102, bf16[1024,4000]{0,1:T(8,128)(2,1)} %param.7), kind=kOutput, calls=%fused_computation.54 | convolution fusion | flops 8388608000 | bytes 26673152 | tf_op jit(solution)/shard_map/dot_general | solution.py:85
  60.1 21.9 %collective-permute-done.3 = bf16[128,4096]{1,0:T(8,128)(2,1)S(1)} collective-permute-done((bf16[128,4096]{1,0:T(8,128)(2,1)S(1)}, bf16[128,4096]{1,0:T(8,128)(2,1)S(1)}, u32[]{:S(2)}, u32[]{:S(2)}) %collective-permute-start.3) | collective-permute-done | bytes 1048608 | tf_op jit(solution)/shard_map/ppermute | solution.py:21
  83.3 4.4 broadcast_in_dim.16
  92.5 13.7 %collective-permute-done.4 = bf16[128,4096]{1,0:T(8,128)(2,1)S(1)} collective-permute-done((bf16[128,4096]{1,0:T(8,128)(2,1)S(1)}, bf16[128,4096]{1,0:T(8,128)(2,1)S(1)}, u32[]{:S(2)}, u32[]{:S(2)}) %collective-permute-start.4) | collective-permute-done | bytes 1048608 | tf_op jit(solution)/shard_map/ppermute | solution.py:21
  106.1 3.0 bitcast_dynamic-update-slice_fusion.5
  109.1 3.2 collective-permute-start.5
  112.4 3.5 collective-permute-start.6
  118.2 20.5 %collective-permute-done.6 = bf16[128,4096]{1,0:T(8,128)(2,1)S(1)} collective-permute-done((bf16[128,4096]{1,0:T(8,128)(2,1)}, bf16[128,4096]{1,0:T(8,128)(2,1)S(1)}, u32[]{:S(2)}, u32[]{:S(2)}) %collective-permute-start.6) | collective-permute-done | bytes 1048608 | tf_op jit(solution)/shard_map/ppermute | solution.py:20
  141.1 4.2 collective-permute-start.8
  147.7 20.0 %collective-permute-done.8 = bf16[128,4096]{1,0:T(8,128)(2,1)S(1)} collective-permute-done((bf16[128,4096]{1,0:T(8,128)(2,1)S(1)}, bf16[128,4096]{1,0:T(8,128)(2,1)S(1)}, u32[]{:S(2)}, u32[]{:S(2)}) %collective-permute-start.8) | collective-permute-done | bytes 1048608 | tf_op jit(solution)/shard_map/ppermute | solution.py:20
  173.1 40.8 %fusion.20 = (f32[1024]{0:T(1024)S(1)}, f32[1024,4000]{0,1:T(8,128)S(1)}) fusion(bf16[1024,4096]{1,0:T(8,128)(2,1)} %bitcast.12, bf16[1,4096,4000]{1,2,0:T(8,128)(2,1)} %param.5), kind=kOutput, calls=%fused_computation.53 | convolution fusion | flops 33558528000 | bytes 57544704 | tf_op jit(solution)/shard_map/dot_general | solution.py:89
  213.9 3.6 fusion.2
  220.5 8.5 %shard_map.67 = f32[8,3,1024]{2,1,0:T(4,128)} custom-call(f32[3,1024]{1,0:T(4,128)} %pad_maximum_fusion.own_ref), custom_call_target="tpu_custom_call" | custom-call | tf_op jit(solution)/shard_map/pallas_call | solution.py:68
  230.2 11.5 %subtract_multiply_fusion = f32[1024,4000]{0,1:T(8,128)} fusion(f32[1024,4000]{0,1:T(8,128)} %copy-done, f32[1024]{0:T(1024)S(1)} %get-tuple-element.28, f32[1024]{0:T(1024)S(1)} %get-tuple-element.27), kind=kLoop, calls=%fused_computation.2 | loop fusion | flops 8192000 | bytes 32776192 | tf_op jit(solution)/shard_map/mul | solution.py:99
  243.6 7.0 %all-reduce = f32[1024]{0:T(1024)S(1)} all-reduce(f32[1024]{0:T(1024)S(1)} %get-tuple-element.27), channel_id=4, replica_groups=mesh['teacher'=4,'vocab'=8] {'teacher'}, use_global_device_ids=true, to_apply=%region_8.9.clone | all-reduce | flops 1024 | bytes 8192
  253.4 139.2 %reduce-scatter.6.cloned.1.call-done = f32[256,4000]{0,1:T(8,128)} async-done(((f32[1024,4000]{0,1:T(8,128)}), f32[256,4000]{0,1:T(8,128)}) %reduce-scatter.6.cloned.1.call-update) | async-done | bytes 4096016 | tf_op jit(solution)/shard_map/reduce_scatter | solution.py:101
  395.3 4.2 multiply_reduce_fusion.1
  400.2 7.7 %shard_map.68 = f32[8,5,256]{2,1,0:T(8,128)} custom-call(f32[5,256]{1,0:T(8,128)} %stack.39.own_ref), custom_call_target="tpu_custom_call" | custom-call | tf_op jit(solution)/shard_map/pallas_call | solution.py:68
  409.6 5.9 subtract_convert_fusion
  415.6 85.6 %all-gather.2.cloned.1.call-done = bf16[1024,4000]{0,1:T(8,128)(2,1)} async-done(((bf16[256,4000]{0,1:T(8,128)(2,1)}), bf16[1024,4000]{0,1:T(8,128)(2,1)}) %all-gather.2.cloned.1.call-update) | async-done | bytes 8192016 | tf_op jit(solution)/shard_map/all_gather | solution.py:122
  501.2 15.0 %fusion.22 = f32[1024,1024]{1,0:T(8,128)} fusion(bf16[1024,4000]{0,1:T(8,128)(2,1)} %all-gather.2.cloned.1.call-done, bf16[1024,4000]{0,1:T(8,128)(2,1)} %param.7), kind=kOutput, calls=%fused_computation.55 | convolution fusion | flops 8388608000 | bytes 20578304 | tf_op jit(solution)/shard_map/dot_general | solution.py:127
  516.1 6.5 %reshape.53 = f32[4,256,2,512]{3,2,1,0:T(2,128)} reshape(f32[1024,1024]{1,0:T(8,128)} %fusion.22) | data formatting | bytes 8388608 | tf_op jit(solution)/shard_map/reshape | solution.py:130
  522.7 5.1 copy.34
  527.8 6.8 %psum.7 = f32[]{:T(128)} all-reduce(f32[]{:T(128)} %get-tuple-element.24), channel_id=1, replica_groups=mesh['teacher'=4,'vocab'=8] {'teacher'}, use_global_device_ids=true, to_apply=%region_20.21 | all-reduce | flops 1 | bytes 8 | tf_op jit(solution)/shard_map/psum | solution.py:123
  535.3 40.6 %reduce-scatter.8.cloned.1.call-done = f32[256,512]{1,0:T(8,128)} async-done(((f32[2048,512]{1,0:T(8,128)}), f32[256,512]{1,0:T(8,128)}) %reduce-scatter.8.cloned.1.call-update) | async-done | bytes 524304 | tf_op jit(solution)/shard_map/reduce_scatter | solution.py:132
  575.9 4.0 collective-permute-start.10
  579.9 14.4 %convolution_bitcast_fusion = f32[1024,4000]{0,1:T(8,128)} fusion(bf16[1024,4000]{0,1:T(8,128)(2,1)} %all-gather.2.cloned.1.call-done, bf16[1024,1024]{1,0:T(8,128)(2,1)S(1)} %bitcast.103), kind=kOutput, calls=%fused_computation.6 | convolution fusion | flops 8388608000 | bytes 26673152 | tf_op jit(solution)/shard_map/dot_general | solution.py:140
  594.2 20.0 %collective-permute-done.10 = f32[256,512]{1,0:T(8,128)S(1)} collective-permute-done((f32[256,512]{1,0:T(8,128)}, f32[256,512]{1,0:T(8,128)S(1)}, u32[]{:S(2)}, u32[]{:S(2)}) %collective-permute-start.10) | collective-permute-done | bytes 524320 | tf_op jit(solution)/shard_map/ppermute | solution.py:139
  (48 shorter events, 39.7 us)
Async XLA Ops:
  11.2 27.3 %all-to-all-start = ((bf16[256,4,1024]{0,2,1:T(8,128)(2,1)}), bf16[256,4,1024]{0,2,1:T(8,128)(2,1)S(1)}, u32[]{:S(2)}, u32[]{:S(2)}) async-start(bf16[256,4,1024]{0,2,1:T(8,128)(2,1)} %bitcast.101), calls=%async_computation | async-start | bytes 4194304 | tf_op jit(solution)/shard_map/all_to_all | solution.py:84
  14.9 226.8 %reduce-scatter.4.cloned.1.call-start = ((), (), s32[]{:S(2)}) async-start(), calls=%async_computation.4 | async-start | bytes 20480000 | tf_op jit(solution)/shard_map/reduce_scatter | solution.py:87
  14.9 41.9 %collective-permute-start = (bf16[128,4096]{1,0:T(8,128)(2,1)}, bf16[128,4096]{1,0:T(8,128)(2,1)}, u32[]{:S(2)}, u32[]{:S(2)}) collective-permute-start(bf16[128,4096]{1,0:T(8,128)(2,1)} %bitcast), channel_id=1, source_target_pairs={{0,2},{1,3},{2,4},{3,5},{4,6},{5,7},{8,10},{9,11},{10,12},{11,13},... | collective-permute-start | bytes 3145736 | tf_op jit(solution)/shard_map/ppermute | solution.py:20
  19.3 37.6 %collective-permute-start.1 = (bf16[128,4096]{1,0:T(8,128)(2,1)}, bf16[128,4096]{1,0:T(8,128)(2,1)S(1)}, u32[]{:S(2)}, u32[]{:S(2)}) collective-permute-start(bf16[128,4096]{1,0:T(8,128)(2,1)} %bitcast), channel_id=1, source_target_pairs={{2,0},{3,1},{4,2},{5,3},{6,4},{7,5},{10,8},{11,9},{12,10},{13,11},... | collective-permute-start | bytes 3145736 | tf_op jit(solution)/shard_map/ppermute | solution.py:21
  56.9 335.8 %reduce-scatter.6.cloned.1.call-start = ((), (), s32[]{:S(2)}) async-start(), calls=%async_computation.5 | async-start | bytes 20480000 | tf_op jit(solution)/shard_map/reduce_scatter | solution.py:101
  56.9 25.1 %collective-permute-start.3 = (bf16[128,4096]{1,0:T(8,128)(2,1)S(1)}, bf16[128,4096]{1,0:T(8,128)(2,1)S(1)}, u32[]{:S(2)}, u32[]{:S(2)}) collective-permute-start(bf16[128,4096]{1,0:T(8,128)(2,1)S(1)} %collective-permute-done.1), channel_id=1, source_target_pairs={{2,0},{3,1},{4,2},{5,3},{6,4},{7,5},{10,8},{11,9},{12,10},{13,11},... | collective-permute-start | bytes 3145736 | tf_op jit(solution)/shard_map/ppermute | solution.py:21
  58.2 31.9 %collective-permute-start.2 = (bf16[128,4096]{1,0:T(8,128)(2,1)}, bf16[128,4096]{1,0:T(8,128)(2,1)}, u32[]{:S(2)}, u32[]{:S(2)}) collective-permute-start(bf16[128,4096]{1,0:T(8,128)(2,1)} %bitcast), channel_id=1, source_target_pairs={{0,1},{1,0},{2,3},{3,2},{4,5},{5,4},{6,7},{7,6},{8,9},{9,8},{10,11... | collective-permute-start | bytes 3145736 | tf_op jit(solution)/shard_map/ppermute | solution.py:30
  82.0 24.1 %collective-permute-start.4 = (bf16[128,4096]{1,0:T(8,128)(2,1)S(1)}, bf16[128,4096]{1,0:T(8,128)(2,1)S(1)}, u32[]{:S(2)}, u32[]{:S(2)}) collective-permute-start(bf16[128,4096]{1,0:T(8,128)(2,1)S(1)} %collective-permute-done.3), channel_id=1, source_target_pairs={{2,0},{3,1},{4,2},{5,3},{6,4},{7,5},{10,8},{11,9},{12,10},{13,11},... | collective-permute-start | bytes 3145736 | tf_op jit(solution)/shard_map/ppermute | solution.py:21
  109.1 6.7 %collective-permute-start.5 = (bf16[128,4096]{1,0:T(8,128)(2,1)}, bf16[128,4096]{1,0:T(8,128)(2,1)}, u32[]{:S(2)}, u32[]{:S(2)}) collective-permute-start(bf16[128,4096]{1,0:T(8,128)(2,1)} %get-tuple-element.34), channel_id=1, source_target_pairs={{0,1},{1,0},{2,3},{3,2},{4,5},{5,4},{6,7},{7,6},{8,9},{9,8},{10,11... | collective-permute-start | bytes 3145736 | tf_op jit(solution)/shard_map/ppermute | solution.py:30
  112.4 26.3 %collective-permute-start.6 = (bf16[128,4096]{1,0:T(8,128)(2,1)}, bf16[128,4096]{1,0:T(8,128)(2,1)S(1)}, u32[]{:S(2)}, u32[]{:S(2)}) collective-permute-start(bf16[128,4096]{1,0:T(8,128)(2,1)} %collective-permute-done), channel_id=1, source_target_pairs={{0,2},{1,3},{2,4},{3,5},{4,6},{5,7},{8,10},{9,11},{10,12},{11,13},... | collective-permute-start | bytes 3145736 | tf_op jit(solution)/shard_map/ppermute | solution.py:20
  140.3 5.0 collective-permute-start.7
  141.1 26.6 %collective-permute-start.8 = (bf16[128,4096]{1,0:T(8,128)(2,1)S(1)}, bf16[128,4096]{1,0:T(8,128)(2,1)S(1)}, u32[]{:S(2)}, u32[]{:S(2)}) collective-permute-start(bf16[128,4096]{1,0:T(8,128)(2,1)S(1)} %collective-permute-done.6), channel_id=1, source_target_pairs={{0,2},{1,3},{2,4},{3,5},{4,6},{5,7},{8,10},{9,11},{10,12},{11,13},... | collective-permute-start | bytes 3145736 | tf_op jit(solution)/shard_map/ppermute | solution.py:20
  169.0 3.1 collective-permute-start.9
  213.9 6.0 copy-start
  241.7 0.7 copy-start.2
  241.8 259.4 %all-gather.2.cloned.1.call-start = ((), (), s32[]{:S(2)}) async-start(), calls=%async_computation.6 | async-start | bytes 10240000 | tf_op jit(solution)/shard_map/all_gather | solution.py:122
  415.5 160.3 %reduce-scatter.8.cloned.1.call-start = ((), (), s32[]{:S(2)}) async-start(), calls=%async_computation.7 | async-start | bytes 4718592 | tf_op jit(solution)/shard_map/reduce_scatter | solution.py:132
  522.7 57.2 %copy-start.1 = (bf16[4,256,1024]{2,1,0:T(8,128)(2,1)S(1)}, bf16[4,256,1024]{2,1,0:T(8,128)(2,1)}, u32[]{:S(2)}) copy-start(bf16[4,256,1024]{2,1,0:T(8,128)(2,1)} %copy.28) | copy-start | bytes 6291460
  575.9 38.4 %collective-permute-start.10 = (f32[256,512]{1,0:T(8,128)}, f32[256,512]{1,0:T(8,128)S(1)}, u32[]{:S(2)}, u32[]{:S(2)}) collective-permute-start(f32[256,512]{1,0:T(8,128)} %reduce-scatter.8.cloned.1.call-done), channel_id=1, source_target_pairs={{0,0},{1,1},{2,8},{3,9},{4,16},{5,17},{6,24},{7,25},{8,2},{9,3},{1... | collective-permute-start | bytes 1572872 | tf_op jit(solution)/shard_map/ppermute | solution.py:139
Sparse Core Ops, SparseCore 0:
  57.0 152.0 reduce-scatter.3
  241.9 150.6 reduce-scatter.5
  415.7 85.4 all-gather.1
  527.9 47.9 reduce-scatter.7

commit v2 on v1

--- a/solution.py
+++ b/solution.py
@@ -19,7 +19,7 @@
     for hop in range(chips - 1):
         up.append(lax.ppermute(up[-1], "vocab", [(i, i + 2) for i in range(nv - 2)]))
         down.append(lax.ppermute(down[-1], "vocab", [(i + 2, i) for i in range(nv - 2)]))
-        if hop == 0:
+        if hop == 1:
             up[-1], down[-1], first = lax.optimization_barrier((up[-1], down[-1], first))
     pair = [(i, i ^ 1) for i in range(nv)]
     rows, width = own.shape
@@ -127,19 +127,27 @@
     gh = lax.dot_general(
         all_grads, student_head, (((1,), (1,)), ((), ())), preferred_element_type=F32
     )
-    gh = gh.reshape(nt, tok // nt, r, feats // r).transpose(0, 2, 1, 3)
-    gh = gh.reshape(nv * (tok // nt), feats // r)
     gh = lax.psum_scatter(gh, "vocab", scatter_dimension=0, tiled=True)
-    swap = [
-        (s * nv + t * r + c, t * nv + s * r + c)
-        for s in range(nt)
-        for t in range(nt)
-        for c in range(r)
-    ]
-    grad_hidden = lax.ppermute(gh, ("teacher", "vocab"), swap)
     grad_weight = lax.dot_general(
         columns, all_grads, (((0,), (0,)), ((), ())), preferred_element_type=F32
     )
+    gh, grad_weight = lax.optimization_barrier((gh, grad_weight))
+    part = lax.rem(lax.axis_index("vocab"), r)
+    rows, width = gh.shape[0], feats // r
+    grad_hidden = jnp.zeros((r, rows, width), F32)
+    for k in range(r):
+        swap = [
+            (s * nv + t * r + h, t * nv + s * r + (h + k) % r)
+            for s in range(nt)
+            for t in range(nt)
+            for h in range(r)
+        ]
+        piece = lax.dynamic_slice(gh, (0, lax.rem(part + k, r) * width), (rows, width))
+        piece = lax.ppermute(piece, ("teacher", "vocab"), swap)
+        grad_hidden = lax.dynamic_update_slice(
+            grad_hidden, piece[None], (lax.rem(part + r - k, r), 0, 0)
+        )
+    grad_hidden = grad_hidden.reshape(r * rows, width)
     return (loss, grad_hidden, grad_weight)
 
 

time: 625 us -> 598 us (0.957)
  waiting for transfers between devices: 382 us -> 360 us
  local copies, waits for them, and re-layouts: 38.1 us -> 24.4 us
  blocking collectives: 13.8 us -> 20.3 us
    all_to_all x1, waiting for transfers between devices: 18 us -> 0.01 us  [per_device(): lax.all_to_all(student_hidden, 'teacher', split_axis=1, concat_axis=0, ti...]
    ppermute x3, waiting for transfers between devices: 35.5 us -> 22.4 us  [gather_hidden(): lax.ppermute(down[-1], 'vocab', [(i + 2, i) for i in range(nv - 2)])]
    reduce_scatter x1, waiting for transfers between devices: 0.01 us -> 12.8 us  [per_device(): lax.psum_scatter(partial_slog, 'teacher', scatter_dimension=0, tiled=True)]
    psum x1, blocking collectives: 6.8 us -> 14.1 us  [per_device(): loss = lax.psum(jnp.sum(kl), 'teacher') / tok]
    reduce_scatter x1, waiting for transfers between devices: 40.6 us -> 33.7 us  [per_device(): gh = lax.psum_scatter(gh, 'vocab', scatter_dimension=0, tiled=True)]
    reshape x1 -> x0, local copies, waits for them, and re-layouts: 6.55 us -> none  [per_device(): gh = gh.reshape(nt, tok // nt, r, feats // r).transpose(0, 2, 1, 3)]
    ppermute x1 -> x2, waiting for transfers between devices: 20 us -> 16.8 us  [per_device(): piece = lax.ppermute(piece, ('teacher', 'vocab'), swap)]
  transfers between devices with their start and end apart: 16 -> 17, of which waited for: 10 -> 13; matrix products, arithmetic and copies ran while one was open for 18% -> 19% of each run, Pallas kernels for 1% -> 1%
where the time goes in v2:
time: 598 us; the launch traced here: 597 us
  waiting for transfers between devices  360 us (60%)
  matrix products  86 us (14%)
  other arithmetic  41.2 us (7%)
  starting transfers between devices  32.2 us (5%)
  local copies, waits for them, and re-layouts  24.4 us (4%)
  blocking collectives  20.3 us (3%)
  between operations  16.4 us (3%)
  Pallas kernels  16 us (3%)
    reduce_scatter x1, waiting for transfers between devices, per_device(): lax.psum_scatter(weighted, 'teacher', scatter_dimension=0, tiled=True)  144 us
    all_gather x1, waiting for transfers between devices, per_device(): all_grads = lax.all_gather(gradl, 'teacher', axis=0, tiled=True)  85.6 us
    dot_general x1, matrix products, per_device(): logits = jnp.dot(hidden, head, preferred_element_type=F32)  40.9 us
    ppermute x3, waiting for transfers between devices, gather_hidden(): lax.ppermute(up[-1], 'vocab', [(i, i + 2) for i in range(nv - 2)])  39.7 us
    reduce_scatter x1, waiting for transfers between devices, per_device(): gh = lax.psum_scatter(gh, 'vocab', scatter_dimension=0, tiled=True)  33.7 us
    ppermute x3, waiting for transfers between devices, gather_hidden(): lax.ppermute(down[-1], 'vocab', [(i + 2, i) for i in range(nv - 2)])  22.4 us
    ppermute x2, waiting for transfers between devices, per_device(): piece = lax.ppermute(piece, ('teacher', 'vocab'), swap)  16.8 us
    pallas_call x2, Pallas kernels, slotted(): pl.pallas_call(functools.partial(exchange_kernel, nv), out_shape=jax.Shap...  16 us
  transfers between devices with their start and end apart: 17, of which 13 were waited for; matrix products, arithmetic and copies ran while one was open for 19% of the time, Pallas kernels for 1%

profile of v2, /device:TPU:3, one launch (start us, length us, event | category | flops | bytes accessed | tf_op | source)
XLA Modules:
  0.0 596.6 jit_solution(12402011640254596515)
XLA Ops:
  7.2 4.1 copy.24
  11.2 3.7 all-to-all-start
  14.9 4.3 collective-permute-start
  20.5 19.4 %collective-permute-done = bf16[128,4096]{1,0:T(8,128)(2,1)} collective-permute-done((bf16[128,4096]{1,0:T(8,128)(2,1)}, bf16[128,4096]{1,0:T(8,128)(2,1)}, u32[]{:S(2)}, u32[]{:S(2)}) %collective-permute-start) | collective-permute-done | bytes 1048608 | tf_op jit(solution)/shard_map/ppermute | solution.py:20
  39.9 5.1 collective-permute-start.1
  48.8 15.8 %fusion.21 = f32[1024,4000]{0,1:T(8,128)} fusion(bf16[1024,1024]{1,0:T(8,128)(2,1)} %bitcast.103, bf16[1024,4000]{0,1:T(8,128)(2,1)} %param.7), kind=kOutput, calls=%fused_computation.58 | convolution fusion | flops 8388608000 | bytes 26673152 | tf_op jit(solution)/shard_map/dot_general | solution.py:85
  64.8 4.6 collective-permute-done.3
  69.4 3.3 collective-permute-start.4
  74.0 4.4 broadcast_in_dim.44
  81.9 17.8 %collective-permute-done.5 = bf16[128,4096]{1,0:T(8,128)(2,1)S(1)} collective-permute-done((bf16[128,4096]{1,0:T(8,128)(2,1)}, bf16[128,4096]{1,0:T(8,128)(2,1)S(1)}, u32[]{:S(2)}, u32[]{:S(2)}) %collective-permute-start.5) | collective-permute-done | bytes 1048608 | tf_op jit(solution)/shard_map/ppermute | solution.py:21
  106.3 2.8 bitcast_dynamic-update-slice_fusion.3
  114.4 20.1 %collective-permute-done.8 = bf16[128,4096]{1,0:T(8,128)(2,1)S(1)} collective-permute-done((bf16[128,4096]{1,0:T(8,128)(2,1)}, bf16[128,4096]{1,0:T(8,128)(2,1)S(1)}, u32[]{:S(2)}, u32[]{:S(2)}) %collective-permute-start.8) | collective-permute-done | bytes 1048608 | tf_op jit(solution)/shard_map/ppermute | solution.py:20
  140.2 40.9 %fusion.20 = (f32[1024]{0:T(1024)S(1)}, f32[1024,4000]{0,1:T(8,128)S(1)}) fusion(bf16[1024,4096]{1,0:T(8,128)(2,1)} %bitcast.12, bf16[1,4096,4000]{1,2,0:T(8,128)(2,1)} %param.5), kind=kOutput, calls=%fused_computation.57 | convolution fusion | flops 33558528000 | bytes 57544704 | tf_op jit(solution)/shard_map/dot_general | solution.py:89
  181.1 3.6 fusion.2
  187.7 8.3 %shard_map.67 = f32[8,3,1024]{2,1,0:T(4,128)} custom-call(f32[3,1024]{1,0:T(4,128)} %pad_maximum_fusion.own_ref), custom_call_target="tpu_custom_call" | custom-call | tf_op jit(solution)/shard_map/pallas_call | solution.py:68
  197.3 11.7 %subtract_multiply_fusion = f32[1024,4000]{0,1:T(8,128)} fusion(f32[1024,4000]{0,1:T(8,128)} %copy-done, f32[1024]{0:T(1024)S(1)} %get-tuple-element.32, f32[1024]{0:T(1024)S(1)} %get-tuple-element.31), kind=kLoop, calls=%fused_computation.2 | loop fusion | flops 8192000 | bytes 32776192 | tf_op jit(solution)/shard_map/mul | solution.py:99
  209.0 12.8 %reduce-scatter.4.cloned.1.call-done = f32[256,4000]{0,1:T(8,128)} async-done(((f32[1024,4000]{0,1:T(8,128)}), f32[256,4000]{0,1:T(8,128)}) %reduce-scatter.4.cloned.1.call-update) | async-done | bytes 4096016 | tf_op jit(solution)/shard_map/reduce_scatter | solution.py:87
  223.1 6.2 %all-reduce = f32[1024]{0:T(1024)S(1)} all-reduce(f32[1024]{0:T(1024)S(1)} %get-tuple-element.31), channel_id=4, replica_groups=mesh['teacher'=4,'vocab'=8] {'teacher'}, use_global_device_ids=true, to_apply=%region_8.9.clone | all-reduce | flops 1024 | bytes 8192
  232.1 144.4 %reduce-scatter.6.cloned.1.call-done = f32[256,4000]{0,1:T(8,128)} async-done(((f32[1024,4000]{0,1:T(8,128)}), f32[256,4000]{0,1:T(8,128)}) %reduce-scatter.6.cloned.1.call-update) | async-done | bytes 4096016 | tf_op jit(solution)/shard_map/reduce_scatter | solution.py:101
  376.5 2.7 fusion.18
  379.2 4.2 multiply_reduce_fusion.1
  384.0 7.7 %shard_map.68 = f32[8,5,256]{2,1,0:T(8,128)} custom-call(f32[5,256]{1,0:T(8,128)} %stack.39.own_ref), custom_call_target="tpu_custom_call" | custom-call | tf_op jit(solution)/shard_map/pallas_call | solution.py:68
  393.5 5.9 subtract_convert_fusion
  399.5 85.6 %all-gather.2.cloned.1.call-done = bf16[1024,4000]{0,1:T(8,128)(2,1)} async-done(((bf16[256,4000]{0,1:T(8,128)(2,1)}), bf16[1024,4000]{0,1:T(8,128)(2,1)}) %all-gather.2.cloned.1.call-update) | async-done | bytes 8192016 | tf_op jit(solution)/shard_map/all_gather | solution.py:122
  485.0 15.0 %fusion.22 = f32[1024,1024]{1,0:T(8,128)} fusion(bf16[1024,4000]{0,1:T(8,128)(2,1)} %all-gather.2.cloned.1.call-done, bf16[1024,4000]{0,1:T(8,128)(2,1)} %param.7), kind=kOutput, calls=%fused_computation.59 | convolution fusion | flops 8388608000 | bytes 20578304 | tf_op jit(solution)/shard_map/dot_general | solution.py:127
  500.1 14.4 %convolution_bitcast_fusion = f32[1024,4000]{0,1:T(8,128)} fusion(bf16[1024,4000]{0,1:T(8,128)(2,1)} %all-gather.2.cloned.1.call-done, bf16[1024,1024]{1,0:T(8,128)(2,1)S(1)} %bitcast.104), kind=kOutput, calls=%fused_computation.6 | convolution fusion | flops 8388608000 | bytes 26673152 | tf_op jit(solution)/shard_map/dot_general | solution.py:131
  514.4 33.7 %reduce-scatter.8.cloned.1.call-done = f32[128,1024]{1,0:T(8,128)} async-done(((f32[1024,1024]{1,0:T(8,128)}), f32[128,1024]{1,0:T(8,128)}) %reduce-scatter.8.cloned.1.call-update) | async-done | bytes 524304 | tf_op jit(solution)/shard_map/reduce_scatter | solution.py:130
  549.2 3.7 collective-permute-start.10
  552.9 3.6 collective-permute-start.11
  556.5 14.1 %psum.7 = f32[]{:T(128)} all-reduce(f32[]{:T(128)} %get-tuple-element.28), channel_id=1, replica_groups=mesh['teacher'=4,'vocab'=8] {'teacher'}, use_global_device_ids=true, to_apply=%region_20.21 | all-reduce | flops 1 | bytes 8 | tf_op jit(solution)/shard_map/psum | solution.py:123
  571.2 10.5 %collective-permute-done.10 = f32[128,512]{1,0:T(8,128)S(1)} collective-permute-done((f32[128,512]{1,0:T(8,128)S(1)}, f32[128,512]{1,0:T(8,128)S(1)}, u32[]{:S(2)}, u32[]{:S(2)}) %collective-permute-start.10) | collective-permute-done | bytes 262176 | tf_op jit(solution)/shard_map/ppermute | solution.py:146
  581.8 6.3 %collective-permute-done.11 = f32[128,512]{1,0:T(8,128)S(1)} collective-permute-done((f32[128,512]{1,0:T(8,128)S(1)}, f32[128,512]{1,0:T(8,128)S(1)}, u32[]{:S(2)}, u32[]{:S(2)}) %collective-permute-start.11) | collective-permute-done | bytes 262176 | tf_op jit(solution)/shard_map/ppermute | solution.py:146
  (53 shorter events, 39.5 us)
Async XLA Ops:
  11.2 35.1 %all-to-all-start = ((bf16[256,4,1024]{0,2,1:T(8,128)(2,1)}), bf16[256,4,1024]{0,2,1:T(8,128)(2,1)S(1)}, u32[]{:S(2)}, u32[]{:S(2)}) async-start(bf16[256,4,1024]{0,2,1:T(8,128)(2,1)} %bitcast.102), calls=%async_computation | async-start | bytes 4194304 | tf_op jit(solution)/shard_map/all_to_all | solution.py:84
  14.9 206.8 %reduce-scatter.4.cloned.1.call-start = ((), (), s32[]{:S(2)}) async-start(), calls=%async_computation.4 | async-start | bytes 20480000 | tf_op jit(solution)/shard_map/reduce_scatter | solution.py:87
  14.9 25.0 %collective-permute-start = (bf16[128,4096]{1,0:T(8,128)(2,1)}, bf16[128,4096]{1,0:T(8,128)(2,1)}, u32[]{:S(2)}, u32[]{:S(2)}) collective-permute-start(bf16[128,4096]{1,0:T(8,128)(2,1)} %bitcast), channel_id=1, source_target_pairs={{0,2},{1,3},{2,4},{3,5},{4,6},{5,7},{8,10},{9,11},{10,12},{11,13},... | collective-permute-start | bytes 3145736 | tf_op jit(solution)/shard_map/ppermute | solution.py:20
  19.2 25.8 %collective-permute-start.2 = (bf16[128,4096]{1,0:T(8,128)(2,1)}, bf16[128,4096]{1,0:T(8,128)(2,1)S(1)}, u32[]{:S(2)}, u32[]{:S(2)}) collective-permute-start(bf16[128,4096]{1,0:T(8,128)(2,1)} %bitcast), channel_id=1, source_target_pairs={{2,0},{3,1},{4,2},{5,3},{6,4},{7,5},{10,8},{11,9},{12,10},{13,11},... | collective-permute-start | bytes 3145736 | tf_op jit(solution)/shard_map/ppermute | solution.py:21
  39.9 24.8 %collective-permute-start.1 = (bf16[128,4096]{1,0:T(8,128)(2,1)}, bf16[128,4096]{1,0:T(8,128)(2,1)}, u32[]{:S(2)}, u32[]{:S(2)}) collective-permute-start(bf16[128,4096]{1,0:T(8,128)(2,1)} %collective-permute-done), channel_id=1, source_target_pairs={{0,2},{1,3},{2,4},{3,5},{4,6},{5,7},{8,10},{9,11},{10,12},{11,13},... | collective-permute-start | bytes 3145736 | tf_op jit(solution)/shard_map/ppermute | solution.py:20
  45.0 24.3 %collective-permute-start.3 = (bf16[128,4096]{1,0:T(8,128)(2,1)S(1)}, bf16[128,4096]{1,0:T(8,128)(2,1)}, u32[]{:S(2)}, u32[]{:S(2)}) collective-permute-start(bf16[128,4096]{1,0:T(8,128)(2,1)S(1)} %collective-permute-done.2), channel_id=1, source_target_pairs={{2,0},{3,1},{4,2},{5,3},{6,4},{7,5},{10,8},{11,9},{12,10},{13,11},... | collective-permute-start | bytes 3145736 | tf_op jit(solution)/shard_map/ppermute | solution.py:21
  69.4 307.1 %reduce-scatter.6.cloned.1.call-start = ((), (), s32[]{:S(2)}) async-start(), calls=%async_computation.5 | async-start | bytes 20480000 | tf_op jit(solution)/shard_map/reduce_scatter | solution.py:101
  69.4 11.4 %collective-permute-start.4 = (bf16[128,4096]{1,0:T(8,128)(2,1)}, bf16[128,4096]{1,0:T(8,128)(2,1)S(1)}, u32[]{:S(2)}, u32[]{:S(2)}) collective-permute-start(bf16[128,4096]{1,0:T(8,128)(2,1)} %bitcast), channel_id=1, source_target_pairs={{0,1},{1,0},{2,3},{3,2},{4,5},{5,4},{6,7},{7,6},{8,9},{9,8},{10,11... | collective-permute-start | bytes 3145736 | tf_op jit(solution)/shard_map/ppermute | solution.py:30
  72.7 26.9 %collective-permute-start.5 = (bf16[128,4096]{1,0:T(8,128)(2,1)}, bf16[128,4096]{1,0:T(8,128)(2,1)S(1)}, u32[]{:S(2)}, u32[]{:S(2)}) collective-permute-start(bf16[128,4096]{1,0:T(8,128)(2,1)} %collective-permute-done.3), channel_id=1, source_target_pairs={{2,0},{3,1},{4,2},{5,3},{6,4},{7,5},{10,8},{11,9},{12,10},{13,11},... | collective-permute-start | bytes 3145736 | tf_op jit(solution)/shard_map/ppermute | solution.py:21
  102.3 3.0 collective-permute-start.6
  109.2 2.9 collective-permute-start.7
  109.6 25.0 %collective-permute-start.8 = (bf16[128,4096]{1,0:T(8,128)(2,1)}, bf16[128,4096]{1,0:T(8,128)(2,1)S(1)}, u32[]{:S(2)}, u32[]{:S(2)}) collective-permute-start(bf16[128,4096]{1,0:T(8,128)(2,1)} %collective-permute-done.1), channel_id=1, source_target_pairs={{0,2},{1,3},{2,4},{3,5},{4,6},{5,7},{8,10},{9,11},{10,12},{11,13},... | collective-permute-start | bytes 3145736 | tf_op jit(solution)/shard_map/ppermute | solution.py:20
  135.9 3.2 collective-permute-start.9
  181.1 6.0 %copy-start = (f32[1024,4000]{0,1:T(8,128)}, f32[1024,4000]{0,1:T(8,128)S(1)}, u32[]{:S(2)}) copy-start(f32[1024,4000]{0,1:T(8,128)S(1)} %get-tuple-element.51) | copy-start | bytes 49152004
  209.0 12.9 %copy-start.3 = (u32[32]{0:T(128)S(1)}, u32[32]{0:T(128)}, u32[]{:S(2)}) copy-start(u32[32]{0:T(128)} %constant.77) | copy-start | bytes 388
  221.8 263.2 %all-gather.2.cloned.1.call-start = ((), (), s32[]{:S(2)}) async-start(), calls=%async_computation.6 | async-start | bytes 10240000 | tf_op jit(solution)/shard_map/all_gather | solution.py:122
  399.4 100.7 %copy-start.1 = (bf16[4,256,1024]{2,1,0:T(8,128)(2,1)S(1)}, bf16[4,256,1024]{2,1,0:T(8,128)(2,1)}, u32[]{:S(2)}) copy-start(bf16[4,256,1024]{2,1,0:T(8,128)(2,1)} %copy.25) | copy-start | bytes 6291460
  399.4 148.7 %reduce-scatter.8.cloned.1.call-start = ((), (), s32[]{:S(2)}) async-start(), calls=%async_computation.7 | async-start | bytes 4718592 | tf_op jit(solution)/shard_map/reduce_scatter | solution.py:130
  549.2 32.6 %collective-permute-start.10 = (f32[128,512]{1,0:T(8,128)S(1)}, f32[128,512]{1,0:T(8,128)S(1)}, u32[]{:S(2)}, u32[]{:S(2)}) collective-permute-start(f32[128,512]{1,0:T(8,128)S(1)} %get-tuple-element.40), channel_id=1, source_target_pairs={{0,0},{1,1},{2,8},{3,9},{4,16},{5,17},{6,24},{7,25},{8,2},{9,3},{1... | collective-permute-start | bytes 786440 | tf_op jit(solution)/shard_map/ppermute | solution.py:146
  552.9 35.2 %collective-permute-start.11 = (f32[128,512]{1,0:T(8,128)S(1)}, f32[128,512]{1,0:T(8,128)S(1)}, u32[]{:S(2)}, u32[]{:S(2)}) collective-permute-start(f32[128,512]{1,0:T(8,128)S(1)} %get-tuple-element.39), channel_id=1, source_target_pairs={{0,1},{1,0},{2,9},{3,8},{4,17},{5,16},{6,25},{7,24},{8,3},{9,2},{1... | collective-permute-start | bytes 786440 | tf_op jit(solution)/shard_map/ppermute | solution.py:146
  588.2 0.8 copy-start.2
Sparse Core Ops, SparseCore 0:
  69.5 152.2 reduce-scatter.3
  225.9 150.5 reduce-scatter.5
  399.5 85.4 all-gather.1
  500.2 47.9 reduce-scatter.7

commit v3 on v2

--- a/solution.py
+++ b/solution.py
@@ -121,6 +121,7 @@
     gradl = (jnp.exp(slog - lse_s[:, None]) - jnp.exp(raw - lse_r[:, None])).astype(jnp.bfloat16)
     all_grads = lax.all_gather(gradl, "teacher", axis=0, tiled=True)
     loss = lax.psum(jnp.sum(kl), "teacher") / tok
+    all_grads, loss = lax.optimization_barrier((all_grads, loss))
 
     r = nv // nt
     feats = student_head.shape[0]

time: 598 us -> 598 us (level)
  blocking collectives: 20.3 us -> 12.9 us
  waiting for transfers between devices: 360 us -> 367 us
    ppermute x2, waiting for transfers between devices: 16.8 us -> 31.5 us  [per_device(): piece = lax.ppermute(piece, ('teacher', 'vocab'), swap)]
    psum x1, blocking collectives: 14.1 us -> 6.67 us  [per_device(): loss = lax.psum(jnp.sum(kl), 'teacher') / tok]
    all_gather x1, waiting for transfers between devices: 85.6 us -> 78.2 us  [per_device(): all_grads = lax.all_gather(gradl, 'teacher', axis=0, tiled=True)]
where the time goes in v3:
time: 598 us; the launch traced here: 597 us
  waiting for transfers between devices  367 us (61%)
  matrix products  86 us (14%)
  other arithmetic  41.2 us (7%)
  starting transfers between devices  32.2 us (5%)
  local copies, waits for them, and re-layouts  24.4 us (4%)
  between operations  16.4 us (3%)
  Pallas kernels  16 us (3%)
  blocking collectives  12.9 us (2%)
    reduce_scatter x1, waiting for transfers between devices, per_device(): lax.psum_scatter(weighted, 'teacher', scatter_dimension=0, tiled=True)  144 us
    all_gather x1, waiting for transfers between devices, per_device(): all_grads = lax.all_gather(gradl, 'teacher', axis=0, tiled=True)  78.2 us
    dot_general x1, matrix products, per_device(): logits = jnp.dot(hidden, head, preferred_element_type=F32)  40.9 us
    ppermute x3, waiting for transfers between devices, gather_hidden(): lax.ppermute(up[-1], 'vocab', [(i, i + 2) for i in range(nv - 2)])  39.7 us
    reduce_scatter x1, waiting for transfers between devices, per_device(): gh = lax.psum_scatter(gh, 'vocab', scatter_dimension=0, tiled=True)  33.7 us
    ppermute x2, waiting for transfers between devices, per_device(): piece = lax.ppermute(piece, ('teacher', 'vocab'), swap)  31.5 us
    ppermute x3, waiting for transfers between devices, gather_hidden(): lax.ppermute(down[-1], 'vocab', [(i + 2, i) for i in range(nv - 2)])  22.4 us
    pallas_call x2, Pallas kernels, slotted(): pl.pallas_call(functools.partial(exchange_kernel, nv), out_shape=jax.Shap...  16 us
  transfers between devices with their start and end apart: 17, of which 13 were waited for; matrix products, arithmetic and copies ran while one was open for 19% of the time, Pallas kernels for 1%

profile of v3, /device:TPU:3, one launch (start us, length us, event | category | flops | bytes accessed | tf_op | source)
XLA Modules:
  0.0 596.6 jit_solution(558662401016941429)
XLA Ops:
  7.2 4.1 copy.24
  11.2 3.7 all-to-all-start
  14.9 4.3 collective-permute-start
  20.5 19.4 %collective-permute-done = bf16[128,4096]{1,0:T(8,128)(2,1)} collective-permute-done((bf16[128,4096]{1,0:T(8,128)(2,1)}, bf16[128,4096]{1,0:T(8,128)(2,1)}, u32[]{:S(2)}, u32[]{:S(2)}) %collective-permute-start) | collective-permute-done | bytes 1048608 | tf_op jit(solution)/shard_map/ppermute | solution.py:20
  39.9 5.1 collective-permute-start.1
  48.8 15.8 %fusion.21 = f32[1024,4000]{0,1:T(8,128)} fusion(bf16[1024,1024]{1,0:T(8,128)(2,1)} %bitcast.103, bf16[1024,4000]{0,1:T(8,128)(2,1)} %param.7), kind=kOutput, calls=%fused_computation.58 | convolution fusion | flops 8388608000 | bytes 26673152 | tf_op jit(solution)/shard_map/dot_general | solution.py:85
  64.8 4.6 collective-permute-done.3
  69.4 3.3 collective-permute-start.4
  74.0 4.4 broadcast_in_dim.44
  81.9 17.8 %collective-permute-done.5 = bf16[128,4096]{1,0:T(8,128)(2,1)S(1)} collective-permute-done((bf16[128,4096]{1,0:T(8,128)(2,1)}, bf16[128,4096]{1,0:T(8,128)(2,1)S(1)}, u32[]{:S(2)}, u32[]{:S(2)}) %collective-permute-start.5) | collective-permute-done | bytes 1048608 | tf_op jit(solution)/shard_map/ppermute | solution.py:21
  106.3 2.8 bitcast_dynamic-update-slice_fusion.3
  114.4 20.1 %collective-permute-done.8 = bf16[128,4096]{1,0:T(8,128)(2,1)S(1)} collective-permute-done((bf16[128,4096]{1,0:T(8,128)(2,1)}, bf16[128,4096]{1,0:T(8,128)(2,1)S(1)}, u32[]{:S(2)}, u32[]{:S(2)}) %collective-permute-start.8) | collective-permute-done | bytes 1048608 | tf_op jit(solution)/shard_map/ppermute | solution.py:20
  140.2 40.9 %fusion.20 = (f32[1024]{0:T(1024)S(1)}, f32[1024,4000]{0,1:T(8,128)S(1)}) fusion(bf16[1024,4096]{1,0:T(8,128)(2,1)} %bitcast.12, bf16[1,4096,4000]{1,2,0:T(8,128)(2,1)} %param.5), kind=kOutput, calls=%fused_computation.57 | convolution fusion | flops 33558528000 | bytes 57544704 | tf_op jit(solution)/shard_map/dot_general | solution.py:89
  181.1 3.6 fusion.2
  187.7 8.3 %shard_map.67 = f32[8,3,1024]{2,1,0:T(4,128)} custom-call(f32[3,1024]{1,0:T(4,128)} %pad_maximum_fusion.own_ref), custom_call_target="tpu_custom_call" | custom-call | tf_op jit(solution)/shard_map/pallas_call | solution.py:68
  197.3 11.7 %subtract_multiply_fusion = f32[1024,4000]{0,1:T(8,128)} fusion(f32[1024,4000]{0,1:T(8,128)} %copy-done, f32[1024]{0:T(1024)S(1)} %get-tuple-element.35, f32[1024]{0:T(1024)S(1)} %get-tuple-element.34), kind=kLoop, calls=%fused_computation.2 | loop fusion | flops 8192000 | bytes 32776192 | tf_op jit(solution)/shard_map/mul | solution.py:99
  209.0 12.8 %reduce-scatter.4.cloned.1.call-done = f32[256,4000]{0,1:T(8,128)} async-done(((f32[1024,4000]{0,1:T(8,128)}), f32[256,4000]{0,1:T(8,128)}) %reduce-scatter.4.cloned.1.call-update) | async-done | bytes 4096016 | tf_op jit(solution)/shard_map/reduce_scatter | solution.py:87
  223.1 6.2 %all-reduce = f32[1024]{0:T(1024)S(1)} all-reduce(f32[1024]{0:T(1024)S(1)} %get-tuple-element.34), channel_id=4, replica_groups=mesh['teacher'=4,'vocab'=8] {'teacher'}, use_global_device_ids=true, to_apply=%region_8.9.clone | all-reduce | flops 1024 | bytes 8192
  232.1 144.4 %reduce-scatter.6.cloned.1.call-done = f32[256,4000]{0,1:T(8,128)} async-done(((f32[1024,4000]{0,1:T(8,128)}), f32[256,4000]{0,1:T(8,128)}) %reduce-scatter.6.cloned.1.call-update) | async-done | bytes 4096016 | tf_op jit(solution)/shard_map/reduce_scatter | solution.py:101
  376.5 2.7 fusion.18
  379.2 4.2 multiply_reduce_fusion.1
  384.0 7.7 %shard_map.68 = f32[8,5,256]{2,1,0:T(8,128)} custom-call(f32[5,256]{1,0:T(8,128)} %stack.39.own_ref), custom_call_target="tpu_custom_call" | custom-call | tf_op jit(solution)/shard_map/pallas_call | solution.py:68
  393.5 5.9 subtract_convert_fusion
  399.5 6.7 %psum.7 = f32[]{:T(128)} all-reduce(f32[]{:T(128)} %get-tuple-element.32), channel_id=1, replica_groups=mesh['teacher'=4,'vocab'=8] {'teacher'}, use_global_device_ids=true, to_apply=%region_20.21 | all-reduce | flops 1 | bytes 8 | tf_op jit(solution)/shard_map/psum | solution.py:123
  406.8 78.2 %all-gather.2.cloned.1.call-done = bf16[1024,4000]{0,1:T(8,128)(2,1)} async-done(((bf16[256,4000]{0,1:T(8,128)(2,1)}), bf16[1024,4000]{0,1:T(8,128)(2,1)}) %all-gather.2.cloned.1.call-update) | async-done | bytes 8192016 | tf_op jit(solution)/shard_map/all_gather | solution.py:122
  485.0 15.0 %fusion.22 = f32[1024,1024]{1,0:T(8,128)} fusion(bf16[1024,4000]{0,1:T(8,128)(2,1)} %all-gather.2.cloned.1.call-done, bf16[1024,4000]{0,1:T(8,128)(2,1)} %param.7), kind=kOutput, calls=%fused_computation.59 | convolution fusion | flops 8388608000 | bytes 20578304 | tf_op jit(solution)/shard_map/dot_general | solution.py:128
  500.1 14.4 %convolution_bitcast_fusion = f32[1024,4000]{0,1:T(8,128)} fusion(bf16[1024,4000]{0,1:T(8,128)(2,1)} %all-gather.2.cloned.1.call-done, bf16[1024,1024]{1,0:T(8,128)(2,1)S(1)} %bitcast.104), kind=kOutput, calls=%fused_computation.6 | convolution fusion | flops 8388608000 | bytes 26673152 | tf_op jit(solution)/shard_map/dot_general | solution.py:132
  514.4 33.7 %reduce-scatter.8.cloned.1.call-done = f32[128,1024]{1,0:T(8,128)} async-done(((f32[1024,1024]{1,0:T(8,128)}), f32[128,1024]{1,0:T(8,128)}) %reduce-scatter.8.cloned.1.call-update) | async-done | bytes 524304 | tf_op jit(solution)/shard_map/reduce_scatter | solution.py:131
  549.2 3.7 collective-permute-start.10
  552.9 3.6 collective-permute-start.11
  556.5 25.2 %collective-permute-done.10 = f32[128,512]{1,0:T(8,128)S(1)} collective-permute-done((f32[128,512]{1,0:T(8,128)S(1)}, f32[128,512]{1,0:T(8,128)S(1)}, u32[]{:S(2)}, u32[]{:S(2)}) %collective-permute-start.10) | collective-permute-done | bytes 262176 | tf_op jit(solution)/shard_map/ppermute | solution.py:147
  581.8 6.3 %collective-permute-done.11 = f32[128,512]{1,0:T(8,128)S(1)} collective-permute-done((f32[128,512]{1,0:T(8,128)S(1)}, f32[128,512]{1,0:T(8,128)S(1)}, u32[]{:S(2)}, u32[]{:S(2)}) %collective-permute-start.11) | collective-permute-done | bytes 262176 | tf_op jit(solution)/shard_map/ppermute | solution.py:147
  (53 shorter events, 39.5 us)
Async XLA Ops:
  11.2 35.1 %all-to-all-start = ((bf16[256,4,1024]{0,2,1:T(8,128)(2,1)}), bf16[256,4,1024]{0,2,1:T(8,128)(2,1)S(1)}, u32[]{:S(2)}, u32[]{:S(2)}) async-start(bf16[256,4,1024]{0,2,1:T(8,128)(2,1)} %bitcast.102), calls=%async_computation | async-start | bytes 4194304 | tf_op jit(solution)/shard_map/all_to_all | solution.py:84
  14.9 206.8 %reduce-scatter.4.cloned.1.call-start = ((), (), s32[]{:S(2)}) async-start(), calls=%async_computation.4 | async-start | bytes 20480000 | tf_op jit(solution)/shard_map/reduce_scatter | solution.py:87
  14.9 25.0 %collective-permute-start = (bf16[128,4096]{1,0:T(8,128)(2,1)}, bf16[128,4096]{1,0:T(8,128)(2,1)}, u32[]{:S(2)}, u32[]{:S(2)}) collective-permute-start(bf16[128,4096]{1,0:T(8,128)(2,1)} %bitcast), channel_id=1, source_target_pairs={{0,2},{1,3},{2,4},{3,5},{4,6},{5,7},{8,10},{9,11},{10,12},{11,13},... | collective-permute-start | bytes 3145736 | tf_op jit(solution)/shard_map/ppermute | solution.py:20
  19.2 25.8 %collective-permute-start.2 = (bf16[128,4096]{1,0:T(8,128)(2,1)}, bf16[128,4096]{1,0:T(8,128)(2,1)S(1)}, u32[]{:S(2)}, u32[]{:S(2)}) collective-permute-start(bf16[128,4096]{1,0:T(8,128)(2,1)} %bitcast), channel_id=1, source_target_pairs={{2,0},{3,1},{4,2},{5,3},{6,4},{7,5},{10,8},{11,9},{12,10},{13,11},... | collective-permute-start | bytes 3145736 | tf_op jit(solution)/shard_map/ppermute | solution.py:21
  39.9 24.8 %collective-permute-start.1 = (bf16[128,4096]{1,0:T(8,128)(2,1)}, bf16[128,4096]{1,0:T(8,128)(2,1)}, u32[]{:S(2)}, u32[]{:S(2)}) collective-permute-start(bf16[128,4096]{1,0:T(8,128)(2,1)} %collective-permute-done), channel_id=1, source_target_pairs={{0,2},{1,3},{2,4},{3,5},{4,6},{5,7},{8,10},{9,11},{10,12},{11,13},... | collective-permute-start | bytes 3145736 | tf_op jit(solution)/shard_map/ppermute | solution.py:20
  45.0 24.3 %collective-permute-start.3 = (bf16[128,4096]{1,0:T(8,128)(2,1)S(1)}, bf16[128,4096]{1,0:T(8,128)(2,1)}, u32[]{:S(2)}, u32[]{:S(2)}) collective-permute-start(bf16[128,4096]{1,0:T(8,128)(2,1)S(1)} %collective-permute-done.2), channel_id=1, source_target_pairs={{2,0},{3,1},{4,2},{5,3},{6,4},{7,5},{10,8},{11,9},{12,10},{13,11},... | collective-permute-start | bytes 3145736 | tf_op jit(solution)/shard_map/ppermute | solution.py:21
  69.4 307.1 %reduce-scatter.6.cloned.1.call-start = ((), (), s32[]{:S(2)}) async-start(), calls=%async_computation.5 | async-start | bytes 20480000 | tf_op jit(solution)/shard_map/reduce_scatter | solution.py:101
  69.4 11.4 %collective-permute-start.4 = (bf16[128,4096]{1,0:T(8,128)(2,1)}, bf16[128,4096]{1,0:T(8,128)(2,1)S(1)}, u32[]{:S(2)}, u32[]{:S(2)}) collective-permute-start(bf16[128,4096]{1,0:T(8,128)(2,1)} %bitcast), channel_id=1, source_target_pairs={{0,1},{1,0},{2,3},{3,2},{4,5},{5,4},{6,7},{7,6},{8,9},{9,8},{10,11... | collective-permute-start | bytes 3145736 | tf_op jit(solution)/shard_map/ppermute | solution.py:30
  72.7 26.9 %collective-permute-start.5 = (bf16[128,4096]{1,0:T(8,128)(2,1)}, bf16[128,4096]{1,0:T(8,128)(2,1)S(1)}, u32[]{:S(2)}, u32[]{:S(2)}) collective-permute-start(bf16[128,4096]{1,0:T(8,128)(2,1)} %collective-permute-done.3), channel_id=1, source_target_pairs={{2,0},{3,1},{4,2},{5,3},{6,4},{7,5},{10,8},{11,9},{12,10},{13,11},... | collective-permute-start | bytes 3145736 | tf_op jit(solution)/shard_map/ppermute | solution.py:21
  102.3 3.0 collective-permute-start.6
  109.2 2.9 collective-permute-start.7
  109.6 25.0 %collective-permute-start.8 = (bf16[128,4096]{1,0:T(8,128)(2,1)}, bf16[128,4096]{1,0:T(8,128)(2,1)S(1)}, u32[]{:S(2)}, u32[]{:S(2)}) collective-permute-start(bf16[128,4096]{1,0:T(8,128)(2,1)} %collective-permute-done.1), channel_id=1, source_target_pairs={{0,2},{1,3},{2,4},{3,5},{4,6},{5,7},{8,10},{9,11},{10,12},{11,13},... | collective-permute-start | bytes 3145736 | tf_op jit(solution)/shard_map/ppermute | solution.py:20
  135.9 3.2 collective-permute-start.9
  181.1 6.0 %copy-start = (f32[1024,4000]{0,1:T(8,128)}, f32[1024,4000]{0,1:T(8,128)S(1)}, u32[]{:S(2)}) copy-start(f32[1024,4000]{0,1:T(8,128)S(1)} %get-tuple-element.55) | copy-start | bytes 49152004
  209.0 12.9 %copy-start.3 = (u32[32]{0:T(128)S(1)}, u32[32]{0:T(128)}, u32[]{:S(2)}) copy-start(u32[32]{0:T(128)} %constant.77) | copy-start | bytes 388
  221.8 263.2 %all-gather.2.cloned.1.call-start = ((), (), s32[]{:S(2)}) async-start(), calls=%async_computation.6 | async-start | bytes 10240000 | tf_op jit(solution)/shard_map/all_gather | solution.py:122
  399.4 148.7 %reduce-scatter.8.cloned.1.call-start = ((), (), s32[]{:S(2)}) async-start(), calls=%async_computation.7 | async-start | bytes 4718592 | tf_op jit(solution)/shard_map/reduce_scatter | solution.py:131
  406.8 93.3 %copy-start.1 = (bf16[4,256,1024]{2,1,0:T(8,128)(2,1)S(1)}, bf16[4,256,1024]{2,1,0:T(8,128)(2,1)}, u32[]{:S(2)}) copy-start(bf16[4,256,1024]{2,1,0:T(8,128)(2,1)} %copy.25) | copy-start | bytes 6291460
  549.2 32.5 %collective-permute-start.10 = (f32[128,512]{1,0:T(8,128)S(1)}, f32[128,512]{1,0:T(8,128)S(1)}, u32[]{:S(2)}, u32[]{:S(2)}) collective-permute-start(f32[128,512]{1,0:T(8,128)S(1)} %get-tuple-element.43), channel_id=1, source_target_pairs={{0,0},{1,1},{2,8},{3,9},{4,16},{5,17},{6,24},{7,25},{8,2},{9,3},{1... | collective-permute-start | bytes 786440 | tf_op jit(solution)/shard_map/ppermute | solution.py:147
  552.9 35.2 %collective-permute-start.11 = (f32[128,512]{1,0:T(8,128)S(1)}, f32[128,512]{1,0:T(8,128)S(1)}, u32[]{:S(2)}, u32[]{:S(2)}) collective-permute-start(f32[128,512]{1,0:T(8,128)S(1)} %get-tuple-element.42), channel_id=1, source_target_pairs={{0,1},{1,0},{2,9},{3,8},{4,17},{5,16},{6,25},{7,24},{8,3},{9,2},{1... | collective-permute-start | bytes 786440 | tf_op jit(solution)/shard_map/ppermute | solution.py:147
  588.1 0.8 copy-start.2
Sparse Core Ops, SparseCore 0:
  69.5 152.2 reduce-scatter.3
  225.9 150.5 reduce-scatter.5
  399.5 85.4 all-gather.1
  500.2 47.9 reduce-scatter.7
